TPU v7x, 128 devices: a whole 4x4x4 slice. The times are simulated.
128 devices in a mesh: dp: 2 (over x_hi), pipe: 4 (over z), tensor: 16 (over x_lo, y, core).
Axes of the slice: x: 4 (x_hi: 2, x_lo: 2; x = x_hi * 2 + x_lo), y: 4, z: 4, core: 2. Of those that a mesh axis runs over, the one named last changes fastest.
Arguments:
- inputs: bfloat16 [4, 3072, 8192], P('pipe', 'dp', 'tensor'), may hold values from -6 to 6
- upstream: bfloat16 [4, 3072, 8192], P('pipe', 'dp', 'tensor'), may hold values from -6 to 6
- factor_one: bfloat16 [4, 32, 4, 256, 256], P('pipe', 'tensor'), may hold values from -0.375 to 0.375
- factor_two: bfloat16 [4, 128, 256, 256], P('pipe', 'tensor'), may hold values from -0.375 to 0.375
- factor_three: bfloat16 [4, 128, 256, 256], P('pipe', 'tensor'), may hold values from -0.375 to 0.375
- factor_four: bfloat16 [4, 32, 4, 256, 256], P('pipe', 'tensor'), may hold values from -0.1875 to 0.1875
Outputs:
- y_next: bfloat16 [4, 3072, 8192], P('pipe', 'dp', 'tensor')
- dx_prev: bfloat16 [4, 3072, 8192], P('pipe', 'dp', 'tensor')
- grad_one: float32 [4, 32, 4, 256, 256], P('pipe', 'tensor')
- grad_two: float32 [4, 128, 256, 256], P('pipe', 'tensor')
- grad_three: float32 [4, 128, 256, 256], P('pipe', 'tensor')
- grad_four: float32 [4, 32, 4, 256, 256], P('pipe', 'tensor')
All inputs are finite; a program needn't handle non-finite values.
Results may differ from a plain program's by a relative error of at most 0.0068.
Values may be sent and summed in bfloat16 or wider, within the bound.
No kernel may reach another device: no remote copies, remote signals or barrier semaphores. Data moves between devices by JAX's collectives and lax.ppermute only.
A program may use at most 192 MiB of HBM per device.

v0:
```python
import jax
import jax.numpy as jnp
from jax import lax
from jax.sharding import PartitionSpec as P


def shifted(value, axis, steps):
    count = lax.axis_size(axis)
    leading, last = (max(0, -steps), min(count, count - steps))
    return lax.ppermute(value, axis, [(source, source + steps) for source in range(leading, last)])


def to_peers(blocks, parts):
    rows, local, width = blocks.shape
    inner = width // (parts * local)
    shaped = blocks.reshape(rows, local, parts, local, inner)
    return shaped.transpose(0, 2, 1, 3, 4).reshape(rows, parts, local * local * inner)


def from_peers(received, local):
    rows, parts, flat = received.shape
    inner = flat // (local * local)
    shaped = received.reshape(rows, parts, local, local, inner)
    return shaped.transpose(0, 3, 1, 2, 4).reshape(rows, local, parts * local * inner)


def shards(inputs, upstream, factor_one, factor_two, factor_three, factor_four):
    parts = lax.axis_size("tensor")
    acts = inputs[0]
    grad_out = upstream[0]
    first = factor_one[0]
    second = factor_two[0]
    third = factor_three[0]
    fourth = factor_four[0]
    groups, expand, bsize = (first.shape[0], first.shape[1], first.shape[2])
    local = groups * expand
    rows = acts.shape[0]
    grouped = acts.reshape(rows, groups, bsize)
    lifted = (
        jnp.einsum("tgi,gkij->tgkj", grouped, first, preferred_element_type=jnp.float32)
        .astype(jnp.bfloat16)
        .reshape(rows, local, bsize)
    )
    outbound = to_peers(lifted, parts)
    mixed = from_peers(
        lax.all_to_all(outbound, "tensor", split_axis=1, concat_axis=1, tiled=True), local
    )
    preact = jnp.einsum("tcj,cjn->tcn", mixed, second, preferred_element_type=jnp.float32)
    active = jax.nn.gelu(preact).astype(jnp.bfloat16)
    mixed, preact, active = (mixed, preact, active)
    narrowed = jnp.einsum("tcn,cno->tco", active, third, preferred_element_type=jnp.float32).astype(
        jnp.bfloat16
    )
    outbound = to_peers(narrowed, parts)
    spread = from_peers(
        lax.all_to_all(outbound, "tensor", split_axis=1, concat_axis=1, tiled=True), local
    )
    count = spread.shape[0]
    output = jnp.einsum(
        "tgkr,gkro->tgo",
        spread.reshape(count, groups, expand, bsize),
        fourth,
        preferred_element_type=jnp.float32,
    ).astype(jnp.bfloat16)
    spread, output = (spread, output.reshape(count, groups * bsize))
    y_next = shifted(output[None], "pipe", 1)
    grad_grouped = grad_out.reshape(rows, groups, bsize)
    spread_four = spread.reshape(rows, groups, expand, bsize)
    grad_spread = (
        jnp.einsum("tgo,gkro->tgkr", grad_grouped, fourth, preferred_element_type=jnp.float32)
        .astype(jnp.bfloat16)
        .reshape(rows, local, bsize)
    )
    grad_four = jnp.einsum(
        "tgkr,tgo->gkro", spread_four, grad_grouped, preferred_element_type=jnp.float32
    )
    outbound = to_peers(grad_spread, parts)
    grad_narrow = from_peers(
        lax.all_to_all(outbound, "tensor", split_axis=1, concat_axis=1, tiled=True), local
    )
    grad_active = jnp.einsum("tco,cno->tcn", grad_narrow, third, preferred_element_type=jnp.float32)
    grad_narrow, grad_active = (grad_narrow, grad_active)
    grad_three = jnp.einsum("tcn,tco->cno", active, grad_narrow, preferred_element_type=jnp.float32)
    pulled = jax.vjp(jax.nn.gelu, preact)[1]
    grad_pre = pulled(grad_active)[0].astype(jnp.bfloat16)
    grad_two = jnp.einsum("tcj,tcn->cjn", mixed, grad_pre, preferred_element_type=jnp.float32)
    grad_mixed = jnp.einsum(
        "tcn,cjn->tcj", grad_pre, second, preferred_element_type=jnp.float32
    ).astype(jnp.bfloat16)
    outbound = to_peers(grad_mixed, parts)
    grad_lift = from_peers(
        lax.all_to_all(outbound, "tensor", split_axis=1, concat_axis=1, tiled=True), local
    )
    count = grad_lift.shape[0]
    grad_input = jnp.einsum(
        "tgkj,gkij->tgi",
        grad_lift.reshape(count, groups, expand, bsize),
        first,
        preferred_element_type=jnp.float32,
    ).astype(jnp.bfloat16)
    grad_lift, grad_input = (grad_lift, grad_input.reshape(count, groups * bsize))
    dx_prev = shifted(grad_input[None], "pipe", -1)
    grad_one = jnp.einsum(
        "tgi,tgkj->gkij",
        grouped,
        grad_lift.reshape(rows, groups, expand, bsize),
        preferred_element_type=jnp.float32,
    )
    grad_one, grad_two, grad_three, grad_four = lax.psum(
        (grad_one, grad_two, grad_three, grad_four), "dp"
    )
    return (y_next, dx_prev, grad_one[None], grad_two[None], grad_three[None], grad_four[None])


def solution(mesh):
    return jax.shard_map(
        shards,
        mesh=mesh,
        in_specs=(
            P("pipe", "dp", "tensor"),
            P("pipe", "dp", "tensor"),
            P("pipe", "tensor", None, None, None),
            P("pipe", "tensor", None, None),
            P("pipe", "tensor", None, None),
            P("pipe", "tensor", None, None, None),
        ),
        out_specs=(
            P("pipe", "dp", "tensor"),
            P("pipe", "dp", "tensor"),
            P("pipe", "tensor", None, None, None),
            P("pipe", "tensor", None, None),
            P("pipe", "tensor", None, None),
            P("pipe", "tensor", None, None, None),
        ),
        check_vma=False,
    )
```

profile of v0, /device:TPU:1, one launch (start us, length us, event | category | flops | bytes accessed | tf_op | source)
XLA Modules:
  0.0 716.7 jit_solution(1809731829033732592)
XLA Ops:
  7.2 0.0 copy-start
  7.2 2.4 reshape_squeeze.6
  9.7 6.5 convert_bitcast_fusion.3
  16.1 13.6 %reshape_reshape.14 = bf16[1536,8,16,8,2]{0,4,3,2,1:T(2,128)(2,1)} reshape(bf16[1536,2,4,256]{0,3,2,1:T(8,128)(2,1)} %convert_bitcast_fusion.3) | data formatting | bytes 12582912 | tf_op jit(solution)/shard_map/reshape;reshape | solution.py:16
  29.7 9.5 %copy.53 = bf16[1536,8,16,8,2]{0,2,4,3,1:T(8,128)(2,1)S(1)} copy(bf16[1536,8,16,8,2]{0,4,3,2,1:T(2,128)(2,1)} %reshape_reshape.14) | data formatting | bytes 12582912 | tf_op jit(solution)/shard_map/reshape;reshape | solution.py:16
  39.2 6.1 copy.54
  45.3 7.2 %all-to-all-start = ((bf16[1536,16,128]{0,2,1:T(8,128)(2,1)}), bf16[1536,16,128]{0,2,1:T(8,128)(2,1)}, u32[]{:S(2)}, u32[]{:S(2)}) async-start(bf16[1536,16,128]{0,2,1:T(8,128)(2,1)} %copy.54), calls=%async_computation | async-start | bytes 12582912 | tf_op jit(solution)/shard_map/all_to_all | solution.py:46
  52.6 2.4 reshape_squeeze.7
  55.0 6.2 convert_bitcast_fusion.1
  61.2 13.1 %reshape_reshape.16 = bf16[1536,8,16,8,2]{0,4,3,2,1:T(2,128)(2,1)} reshape(bf16[1536,2,4,256]{0,3,2,1:T(8,128)(2,1)} %convert_bitcast_fusion.1) | data formatting | bytes 12582912 | tf_op jit(solution)/shard_map/reshape;reshape | solution.py:16
  74.3 9.5 %copy.67 = bf16[1536,8,16,8,2]{0,2,4,3,1:T(8,128)(2,1)S(1)} copy(bf16[1536,8,16,8,2]{0,4,3,2,1:T(2,128)(2,1)} %reshape_reshape.16) | data formatting | bytes 12582912 | tf_op jit(solution)/shard_map/reshape;reshape | solution.py:16
  83.8 6.1 copy.68
  89.9 51.1 %all-to-all-done = bf16[1536,16,128]{0,2,1:T(8,128)(2,1)} async-done(((bf16[1536,16,128]{0,2,1:T(8,128)(2,1)}), bf16[1536,16,128]{0,2,1:T(8,128)(2,1)}, u32[]{:S(2)}, u32[]{:S(2)}) %all-to-all-start) | async-done | bytes 6291488 | tf_op jit(solution)/shard_map/all_to_all | solution.py:46
  141.0 12.3 %all-to-all-start.2 = ((bf16[1536,16,128]{0,2,1:T(8,128)(2,1)}), bf16[1536,16,128]{0,2,1:T(8,128)(2,1)}, u32[]{:S(2)}, u32[]{:S(2)}) async-start(bf16[1536,16,128]{0,2,1:T(8,128)(2,1)} %copy.68), calls=%async_computation.2 | async-start | bytes 12582912 | tf_op jit(solution)/shard_map/all_to_all | solution.py:79
  153.3 6.3 copy.55
  159.5 0.0 copy-start.3
  159.6 3.5 copy.56
  163.1 9.2 %fusion.11 = f32[8,1536,256]{2,1,0:T(8,128)} fusion(bf16[1536,8,256]{0,1,2:T(8,128)(2,1)S(1)} %bitcast.136, bf16[1,8,256,256]{3,2,1,0:T(8,128)(2,1)S(1)} %copy-done.3), kind=kOutput, calls=%fused_computation.20 | convolution fusion | flops 1610612736 | bytes 19922944 | tf_op jit(solution)/shard_map/tcj,cjn->tcn/dot_general | solution.py:48
  172.3 9.7 %convert_bitcast_fusion.2 = bf16[1536,8,256]{0,2,1:T(8,128)(2,1)} fusion(bf16[1,8,256,256]{3,2,1,0:T(8,128)(2,1)S(1)} %copy-done, f32[8,1536,256]{2,1,0:T(8,128)} %fusion.11), kind=kOutput, calls=%fused_computation.18 | convolution fusion | flops 1642070016 | bytes 19922944 | tf_op jit(solution)/shard_map/tcn,cno->tco/dot_general | solution.py:51
  182.0 13.1 %reshape.51 = bf16[1536,8,16,8,2]{0,4,3,2,1:T(2,128)(2,1)} reshape(bf16[1536,8,256]{0,2,1:T(8,128)(2,1)} %convert_bitcast_fusion.2) | data formatting | bytes 12582912 | tf_op jit(solution)/shard_map/reshape | solution.py:16
  195.1 9.5 %copy.59 = bf16[1536,8,16,8,2]{0,2,4,3,1:T(8,128)(2,1)S(1)} copy(bf16[1536,8,16,8,2]{0,4,3,2,1:T(2,128)(2,1)} %reshape.51) | data formatting | bytes 12582912 | tf_op jit(solution)/shard_map/reshape | solution.py:16
  204.6 6.2 copy.60
  210.8 30.9 %all-to-all-done.2 = bf16[1536,16,128]{0,2,1:T(8,128)(2,1)} async-done(((bf16[1536,16,128]{0,2,1:T(8,128)(2,1)}), bf16[1536,16,128]{0,2,1:T(8,128)(2,1)}, u32[]{:S(2)}, u32[]{:S(2)}) %all-to-all-start.2) | async-done | bytes 6291488 | tf_op jit(solution)/shard_map/all_to_all | solution.py:79
  241.7 12.1 %all-to-all-start.1 = ((bf16[1536,16,128]{0,2,1:T(8,128)(2,1)}), bf16[1536,16,128]{0,2,1:T(8,128)(2,1)}, u32[]{:S(2)}, u32[]{:S(2)}) async-start(bf16[1536,16,128]{0,2,1:T(8,128)(2,1)} %copy.60), calls=%async_computation.1 | async-start | bytes 12582912 | tf_op jit(solution)/shard_map/all_to_all | solution.py:56
  253.8 6.3 copy.69
  260.1 6.1 copy.70
  266.2 9.1 %copy.71 = bf16[1536,8,256]{2,0,1:T(8,128)(2,1)} copy(bf16[1536,8,256]{0,1,2:T(8,128)(2,1)} %bitcast.143) | data formatting | bytes 12582912 | tf_op jit(solution)/shard_map/reshape | solution.py:24
  275.3 14.1 %fusion.6 = bf16[1536,8,256]{2,0,1:T(8,128)(2,1)S(1)} fusion(f32[8,1536,256]{2,1,0:T(8,128)} %fusion.11, bf16[1536,8,256]{2,0,1:T(8,128)(2,1)} %copy.71, bf16[1,8,256,256]{3,2,1,0:T(8,128)(2,1)S(1)} %copy-done), kind=kOutput, calls=%fused_computation.8 | convolution fusion | flops 1673527296 | bytes 26214400 | tf_op jit(solution)/shard_map/tco,cno->tcn/dot_general | solution.py:81
  289.4 2.6 copy-done.4
  292.0 4.5 convert_bitcast_fusion
  296.4 13.3 %reshape.57 = bf16[1536,8,16,8,2]{0,4,3,2,1:T(2,128)(2,1)} reshape(bf16[1536,8,256]{0,2,1:T(8,128)(2,1)} %convert_bitcast_fusion) | data formatting | bytes 12582912 | tf_op jit(solution)/shard_map/reshape | solution.py:16
  309.7 9.5 %copy.72 = bf16[1536,8,16,8,2]{0,2,4,3,1:T(8,128)(2,1)S(1)} copy(bf16[1536,8,16,8,2]{0,4,3,2,1:T(2,128)(2,1)} %reshape.57) | data formatting | bytes 12582912 | tf_op jit(solution)/shard_map/reshape | solution.py:16
  319.2 6.1 copy.73
  325.3 16.9 %all-to-all-done.1 = bf16[1536,16,128]{0,2,1:T(8,128)(2,1)} async-done(((bf16[1536,16,128]{0,2,1:T(8,128)(2,1)}), bf16[1536,16,128]{0,2,1:T(8,128)(2,1)}, u32[]{:S(2)}, u32[]{:S(2)}) %all-to-all-start.1) | async-done | bytes 6291488 | tf_op jit(solution)/shard_map/all_to_all | solution.py:56
  342.2 11.7 %all-to-all-start.3 = ((bf16[1536,16,128]{0,2,1:T(8,128)(2,1)}), bf16[1536,16,128]{0,2,1:T(8,128)(2,1)}, u32[]{:S(2)}, u32[]{:S(2)}) async-start(bf16[1536,16,128]{0,2,1:T(8,128)(2,1)} %copy.73), calls=%async_computation.3 | async-start | bytes 12582912 | tf_op jit(solution)/shard_map/all_to_all | solution.py:92
  354.0 0.2 all-reduce.3.cloned.1.call-start
  354.2 8.2 %fusion.17 = f32[1,8,256,256]{3,2,1,0:T(8,128)} fusion(bf16[1536,8,256]{2,0,1:T(8,128)(2,1)} %copy-done.4, bf16[1536,8,256]{0,1,2:T(8,128)(2,1)} %bitcast.137), kind=kOutput, calls=%fused_computation.28 | convolution fusion | flops 1610612736 | bytes 14680064 | tf_op jit(solution)/shard_map/tcj,tcn->cjn/dot_general | solution.py:86
  362.4 12.5 %convolution_bitcast_fusion.3 = f32[1,8,256,256]{3,2,1,0:T(8,128)} fusion(bf16[1536,8,256]{2,0,1:T(8,128)(2,1)} %copy.71, f32[8,1536,256]{2,1,0:T(8,128)} %fusion.11), kind=kOutput, calls=%fused_computation.30 | convolution fusion | flops 1638924288 | bytes 20971520 | tf_op jit(solution)/shard_map/tcn,tco->cno/dot_general | solution.py:83
  375.0 6.3 copy.61
  381.2 7.4 %copy.62 = bf16[1536,8,16,8,2]{0,4,3,2,1:T(2,128)(2,1)} copy(bf16[1536,8,16,8,2]{0,2,4,1,3:T(8,128)(2,1)S(1)} %bitcast.145) | data formatting | bytes 12582912 | tf_op jit(solution)/shard_map/transpose | solution.py:24
  388.7 13.6 %reshape_reshape.15 = bf16[1536,2,4,256]{0,3,2,1:T(8,128)(2,1)} reshape(bf16[1536,8,16,8,2]{0,4,3,2,1:T(2,128)(2,1)} %copy.62) | data formatting | bytes 12582912 | tf_op jit(solution)/shard_map/reshape;reshape | solution.py:61
  402.3 40.2 %all-to-all-done.3 = bf16[1536,16,128]{0,2,1:T(8,128)(2,1)} async-done(((bf16[1536,16,128]{0,2,1:T(8,128)(2,1)}), bf16[1536,16,128]{0,2,1:T(8,128)(2,1)}, u32[]{:S(2)}, u32[]{:S(2)}) %all-to-all-start.3) | async-done | bytes 6291488 | tf_op jit(solution)/shard_map/all_to_all | solution.py:92
  442.5 6.3 copy.74
  448.8 7.1 copy.75
  455.9 13.7 %reshape_reshape.17 = bf16[1536,2,4,256]{0,3,2,1:T(8,128)(2,1)} reshape(bf16[1536,8,16,8,2]{0,4,3,2,1:T(2,128)(2,1)} %copy.75) | data formatting | bytes 12582912 | tf_op jit(solution)/shard_map/reshape;reshape | solution.py:97
  469.6 6.0 convolution_bitcast_fusion.4
  475.6 5.9 convolution_bitcast_fusion.2
  481.5 0.0 all-reduce.3.cloned.1.call-update
  481.6 1.2 copy-done.13
  482.8 4.6 fusion.15
  487.4 1.6 copy.65
  489.0 3.6 collective-permute-start
  492.6 6.1 fusion.16
  498.7 2.8 copy.77
  501.5 1.3 collective-permute-start.1
  502.8 22.9 %collective-permute-done = bf16[1,1536,512]{2,1,0:T(8,128)(2,1)S(1)} collective-permute-done((bf16[1,1536,512]{2,1,0:T(8,128)(2,1)}, bf16[1,1536,512]{2,1,0:T(8,128)(2,1)S(1)}, u32[]{:S(2)}, u32[]{:S(2)}) %collective-permute-start) | collective-permute-done | bytes 1572896 | tf_op jit(solution)/shard_map/ppermute | solution.py:10
  525.6 13.1 %collective-permute-done.1 = bf16[1,1536,512]{2,1,0:T(8,128)(2,1)} collective-permute-done((bf16[1,1536,512]{2,1,0:T(8,128)(2,1)}, bf16[1,1536,512]{2,1,0:T(8,128)(2,1)}, u32[]{:S(2)}, u32[]{:S(2)}) %collective-permute-start.1) | collective-permute-done | bytes 1572896 | tf_op jit(solution)/shard_map/ppermute | solution.py:10
  538.7 158.1 %all-reduce.3.cloned.1.call-done = (f32[1,2,4,256,256]{3,4,2,1,0:T(8,128)}, f32[1,8,256,256]{3,2,1,0:T(8,128)}, f32[1,8,256,256]{3,2,1,0:T(8,128)}, f32[1,2,4,256,256]{4,3,2,1,0:T(8,128)}) async-done(((f32[1,2,4,256,256]{3,4,2,1,0:T(8,128)}, f32[1,8,256,256]{3,2,1,0:T(8,128)}, f32[1,8,256,256]{3,2,1,0:T(8,128)}, f32[1,2,4,256,256]{4,3,2,1,0:T(8,128)}), (f32[1,2,4,256,256]{3,4,2,1,0:T(8,128)}, ...) | async-done | bytes 8388624 | tf_op jit(solution)/shard_map/psum | solution.py:109
  696.8 3.0 copy.83
  699.9 2.8 copy.124
  702.7 2.8 copy.125
  705.5 1.3 copy.126
  706.8 1.3 copy.127
  708.1 1.3 copy.128
  (24 shorter events, 0.1 us)
Async XLA Ops:
  7.2 165.1 %copy-start = (bf16[1,8,256,256]{3,2,1,0:T(8,128)(2,1)S(1)}, bf16[1,8,256,256]{3,2,1,0:T(8,128)(2,1)}, u32[]{:S(2)}) copy-start(bf16[1,8,256,256]{3,2,1,0:T(8,128)(2,1)} %param.10) | copy-start | bytes 3145732
  9.6 20.1 %copy-start.5 = (bf16[1536,2,256]{2,1,0:T(2,128)(2,1)}, bf16[1536,2,256]{2,1,0:T(2,128)(2,1)S(1)}, u32[]{:S(2)}) copy-start(bf16[1536,2,256]{2,1,0:T(2,128)(2,1)S(1)} %reshape_squeeze.6) | copy-start | bytes 4718596
  45.3 95.7 %all-to-all-start = ((bf16[1536,16,128]{0,2,1:T(8,128)(2,1)}), bf16[1536,16,128]{0,2,1:T(8,128)(2,1)}, u32[]{:S(2)}, u32[]{:S(2)}) async-start(bf16[1536,16,128]{0,2,1:T(8,128)(2,1)} %copy.54), calls=%async_computation | async-start | bytes 12582912 | tf_op jit(solution)/shard_map/all_to_all | solution.py:46
  54.9 19.4 %copy-start.7 = (bf16[1536,2,256]{2,1,0:T(2,128)(2,1)}, bf16[1536,2,256]{2,1,0:T(2,128)(2,1)S(1)}, u32[]{:S(2)}) copy-start(bf16[1536,2,256]{2,1,0:T(2,128)(2,1)S(1)} %reshape_squeeze.7) | copy-start | bytes 4718596
  141.0 100.7 %all-to-all-start.2 = ((bf16[1536,16,128]{0,2,1:T(8,128)(2,1)}), bf16[1536,16,128]{0,2,1:T(8,128)(2,1)}, u32[]{:S(2)}, u32[]{:S(2)}) async-start(bf16[1536,16,128]{0,2,1:T(8,128)(2,1)} %copy.68), calls=%async_computation.2 | async-start | bytes 12582912 | tf_op jit(solution)/shard_map/all_to_all | solution.py:79
  159.5 3.5 copy-start.3
  163.0 9.3 %copy-start.2 = (bf16[1536,8,16,8,2]{0,1,4,3,2:T(8,128)(2,1)}, bf16[1536,8,16,8,2]{0,1,4,3,2:T(8,128)(2,1)S(1)}, u32[]{:S(2)}) copy-start(bf16[1536,8,16,8,2]{0,1,4,3,2:T(8,128)(2,1)S(1)} %copy.56) | copy-start | bytes 18874372
  241.7 100.5 %all-to-all-start.1 = ((bf16[1536,16,128]{0,2,1:T(8,128)(2,1)}), bf16[1536,16,128]{0,2,1:T(8,128)(2,1)}, u32[]{:S(2)}, u32[]{:S(2)}) async-start(bf16[1536,16,128]{0,2,1:T(8,128)(2,1)} %copy.60), calls=%async_computation.1 | async-start | bytes 12582912 | tf_op jit(solution)/shard_map/all_to_all | solution.py:56
  289.4 2.6 copy-start.4
  342.2 100.3 %all-to-all-start.3 = ((bf16[1536,16,128]{0,2,1:T(8,128)(2,1)}), bf16[1536,16,128]{0,2,1:T(8,128)(2,1)}, u32[]{:S(2)}, u32[]{:S(2)}) async-start(bf16[1536,16,128]{0,2,1:T(8,128)(2,1)} %copy.73), calls=%async_computation.3 | async-start | bytes 12582912 | tf_op jit(solution)/shard_map/all_to_all | solution.py:92
  354.0 342.9 %all-reduce.3.cloned.1.call-start = ((), (), s32[]{:S(2)}) async-start(), calls=%async_computation.4 | async-start | bytes 16777216 | tf_op jit(solution)/shard_map/psum | solution.py:109
  455.9 13.7 %copy-start.6 = (bf16[1536,2,256]{2,1,0:T(2,128)(2,1)S(1)}, bf16[1536,2,256]{2,1,0:T(2,128)(2,1)}, u32[]{:S(2)}) copy-start(bf16[1536,2,256]{2,1,0:T(2,128)(2,1)} %copy-done.5) | copy-start | bytes 4718596
  469.6 6.0 copy-start.8
  481.5 1.2 copy-start.13
  489.0 36.7 %collective-permute-start = (bf16[1,1536,512]{2,1,0:T(8,128)(2,1)}, bf16[1,1536,512]{2,1,0:T(8,128)(2,1)S(1)}, u32[]{:S(2)}, u32[]{:S(2)}) collective-permute-start(bf16[1,1536,512]{2,1,0:T(8,128)(2,1)} %copy.65), channel_id=1, source_target_pairs={{0,16},{16,32},{32,48},{1,17},{17,33},{33,49},{2,18},{18,34},{34,5... | collective-permute-start | bytes 4718600 | tf_op jit(solution)/shard_map/ppermute | solution.py:10
  501.5 37.3 %collective-permute-start.1 = (bf16[1,1536,512]{2,1,0:T(8,128)(2,1)}, bf16[1,1536,512]{2,1,0:T(8,128)(2,1)}, u32[]{:S(2)}, u32[]{:S(2)}) collective-permute-start(bf16[1,1536,512]{2,1,0:T(8,128)(2,1)} %copy.77), channel_id=1, source_target_pairs={{16,0},{32,16},{48,32},{17,1},{33,17},{49,33},{18,2},{34,18},{50,3... | collective-permute-start | bytes 4718600 | tf_op jit(solution)/shard_map/ppermute | solution.py:10
  525.6 13.1 %copy-start.12 = (bf16[1,1536,512]{2,1,0:T(8,128)(2,1)}, bf16[1,1536,512]{2,1,0:T(8,128)(2,1)S(1)}, u32[]{:S(2)}) copy-start(bf16[1,1536,512]{2,1,0:T(8,128)(2,1)S(1)} %collective-permute-done) | copy-start | bytes 4718596
  696.8 8.6 %copy-start.11 = (f32[1,8,256,256]{3,2,1,0:T(8,128)S(1)}, f32[1,8,256,256]{3,2,1,0:T(8,128)}, u32[]{:S(2)}) copy-start(f32[1,8,256,256]{3,2,1,0:T(8,128)} %get-tuple-element.37) | copy-start | bytes 6291460
  699.9 6.9 copy-start.10
  702.7 5.5 copy-start.9
  702.7 6.8 copy-start.1
Sparse Core Ops, SparseCore 0:
  481.7 215.1 all-reduce.2
where the time goes:
time: 723 us; the launch traced here: 717 us
  waiting for transfers between devices  333 us (46%)
  local copies, waits for them, and re-layouts  227 us (31%)
  matrix products  93.5 us (13%)
  starting transfers between devices  48.5 us (7%)
  between operations  14.7 us (2%)
    psum x1, waiting for transfers between devices, shards(): lax.psum((grad_one, grad_two, grad_three, grad_four), 'dp')  158 us
    all_to_all x4, waiting for transfers between devices, shards(): lax.all_to_all(outbound, 'tensor', split_axis=1, concat_axis=1, tiled=True)  139 us
    another operation x4, local copies, waits for them, and re-layouts, to_peers(): shaped = blocks.reshape(rows, local, parts, local, inner)  45.6 us
    reshape x4, local copies, waits for them, and re-layouts, to_peers(): shaped = blocks.reshape(rows, local, parts, local, inner)  45.3 us
    all_to_all x4, starting transfers between devices, shards(): lax.all_to_all(outbound, 'tensor', split_axis=1, concat_axis=1, tiled=True)  43.3 us
    ppermute x2, waiting for transfers between devices, shifted(): lax.ppermute(value, axis, [(source, source + steps) for source in range(l...  36 us
    all_to_all x4, local copies, waits for them, and re-layouts, shards(): lax.all_to_all(outbound, 'tensor', split_axis=1, concat_axis=1, tiled=True)  25 us
    reshape x4, local copies, waits for them, and re-layouts, to_peers(): shaped.transpose(0, 2, 1, 3, 4).reshape(rows, parts, local * local * inner)  24.6 us
  transfers between devices with their start and end apart: 7, of which 7 were waited for; matrix products, arithmetic and copies ran while one was open for 32% of the time, Pallas kernels for 0%

commit v1 on v0

--- a/solution.py
+++ b/solution.py
@@ -89,7 +89,13 @@
     ).astype(jnp.bfloat16)
     outbound = to_peers(grad_mixed, parts)
     grad_lift = from_peers(
-        lax.all_to_all(outbound, "tensor", split_axis=1, concat_axis=1, tiled=True), local
+        jnp.concatenate(
+            lax.all_to_all(
+                jnp.stack(jnp.split(outbound, lax.axis_size("tensor"), axis=1)), "tensor", 0, 0
+            ),
+            axis=1,
+        ),
+        local,
     )
     count = grad_lift.shape[0]
     grad_input = jnp.einsum(

time: 723 us -> 829 us (1.15)
  local copies, waits for them, and re-layouts: 227 us -> 318 us
  waiting for transfers between devices: 333 us -> 346 us
    split x0 -> x17, local copies, waits for them, and re-layouts: none -> 65.2 us  [shards(): jnp.split(outbound, lax.axis_size('tensor'), axis=1)]
    all_to_all x0 -> x1, waiting for transfers between devices: none -> 34.2 us  [shards(): lax.all_to_all(jnp.stack(jnp.split(outbound, lax.axis_size('tensor'), axi...]
    all_to_all x4 -> x3, waiting for transfers between devices: 139 us -> 118 us  [shards(): lax.all_to_all(outbound, 'tensor', split_axis=1, concat_axis=1, tiled=True)]
    unnamed x34 -> x59, local copies, waits for them, and re-layouts: 16.4 us -> 36.6 us
    all_to_all x4 -> x3, starting transfers between devices: 43.3 us -> 31.6 us  [shards(): lax.all_to_all(outbound, 'tensor', split_axis=1, concat_axis=1, tiled=True)]
    all_to_all x0 -> x1, starting transfers between devices: none -> 11.4 us  [shards(): lax.all_to_all(jnp.stack(jnp.split(outbound, lax.axis_size('tensor'), axi...]
    reshape x0 -> x1, local copies, waits for them, and re-layouts: none -> 9.06 us  [shards(): jnp.concatenate(lax.all_to_all(jnp.stack(jnp.split(outbound, lax.axis_siz...]
    reshape x4 -> x3, local copies, waits for them, and re-layouts: 24.6 us -> 18.3 us  [to_peers(): shaped.transpose(0, 2, 1, 3, 4).reshape(rows, parts, local * local * inner)]
  transfers between devices with their start and end apart: 7 -> 7, of which waited for: 7 -> 6; matrix products, arithmetic and copies ran while one was open for 32% -> 26% of each run, Pallas kernels for 0% -> 0%
where the time goes in v1:
time: 829 us; the launch traced here: 822 us
  waiting for transfers between devices  346 us (42%)
  local copies, waits for them, and re-layouts  318 us (38%)
  matrix products  94.8 us (11%)
  starting transfers between devices  48.4 us (6%)
  between operations  14.5 us (2%)
    psum x1, waiting for transfers between devices, shards(): lax.psum((grad_one, grad_two, grad_three, grad_four), 'dp')  158 us
    all_to_all x3, waiting for transfers between devices, shards(): lax.all_to_all(outbound, 'tensor', split_axis=1, concat_axis=1, tiled=True)  118 us
    split x17, local copies, waits for them, and re-layouts, shards(): jnp.split(outbound, lax.axis_size('tensor'), axis=1)  65.2 us
    reshape x4, local copies, waits for them, and re-layouts, to_peers(): shaped = blocks.reshape(rows, local, parts, local, inner)  48.3 us
    another operation x4, local copies, waits for them, and re-layouts, to_peers(): shaped = blocks.reshape(rows, local, parts, local, inner)  45.3 us
    unnamed x59, local copies, waits for them, and re-layouts  36.6 us
    ppermute x2, waiting for transfers between devices, shifted(): lax.ppermute(value, axis, [(source, source + steps) for source in range(l...  36 us
    all_to_all x1, waiting for transfers between devices, shards(): lax.all_to_all(jnp.stack(jnp.split(outbound, lax.axis_size('tensor'), axi...  34.2 us
  transfers between devices with their start and end apart: 7, of which 6 were waited for; matrix products, arithmetic and copies ran while one was open for 26% of the time, Pallas kernels for 0%

profile of v1, /device:TPU:1, one launch (start us, length us, event | category | flops | bytes accessed | tf_op | source)
XLA Modules:
  0.0 821.5 jit_solution(12262878906491480694)
XLA Ops:
  7.2 2.4 reshape_squeeze.7
  9.7 6.3 convert_bitcast_fusion.1
  15.9 13.3 %reshape_reshape.19 = bf16[1536,8,16,8,2]{0,4,3,2,1:T(2,128)(2,1)} reshape(bf16[1536,2,4,256]{0,3,2,1:T(8,128)(2,1)} %convert_bitcast_fusion.1) | data formatting | bytes 12582912 | tf_op jit(solution)/shard_map/reshape;reshape | solution.py:16
  29.2 9.5 %copy.834 = bf16[1536,8,16,8,2]{0,2,4,3,1:T(8,128)(2,1)S(1)} copy(bf16[1536,8,16,8,2]{0,4,3,2,1:T(2,128)(2,1)} %reshape_reshape.19) | data formatting | bytes 12582912 | tf_op jit(solution)/shard_map/reshape;reshape | solution.py:16
  38.7 6.1 copy.835
  44.8 7.3 all-to-all-start.2
  52.1 2.4 reshape_squeeze.6
  54.4 6.5 convert_bitcast_fusion.3
  60.9 13.1 %reshape_reshape.17 = bf16[1536,8,16,8,2]{0,4,3,2,1:T(2,128)(2,1)} reshape(bf16[1536,2,4,256]{0,3,2,1:T(8,128)(2,1)} %convert_bitcast_fusion.3) | data formatting | bytes 12582912 | tf_op jit(solution)/shard_map/reshape;reshape | solution.py:16
  74.0 9.5 %copy.820 = bf16[1536,8,16,8,2]{0,2,4,3,1:T(8,128)(2,1)S(1)} copy(bf16[1536,8,16,8,2]{0,4,3,2,1:T(2,128)(2,1)} %reshape_reshape.17) | data formatting | bytes 12582912 | tf_op jit(solution)/shard_map/reshape;reshape | solution.py:16
  83.5 6.1 copy.821
  89.6 50.9 %all-to-all-done.2 = bf16[1536,16,128]{0,2,1:T(8,128)(2,1)} async-done(((bf16[1536,16,128]{0,2,1:T(8,128)(2,1)}), bf16[1536,16,128]{0,2,1:T(8,128)(2,1)}, u32[]{:S(2)}, u32[]{:S(2)}) %all-to-all-start.2) | async-done | bytes 6291488 | tf_op jit(solution)/shard_map/all_to_all | solution.py:79
  140.5 12.3 %all-to-all-start = ((bf16[1536,16,128]{0,2,1:T(8,128)(2,1)}), bf16[1536,16,128]{0,2,1:T(8,128)(2,1)}, u32[]{:S(2)}, u32[]{:S(2)}) async-start(bf16[1536,16,128]{0,2,1:T(8,128)(2,1)} %copy.821), calls=%async_computation | async-start | bytes 12582912 | tf_op jit(solution)/shard_map/all_to_all | solution.py:46
  152.8 6.3 copy.836
  159.0 6.1 copy.837
  165.1 9.3 %copy.838 = bf16[1536,8,256]{2,0,1:T(8,128)(2,1)} copy(bf16[1536,8,256]{0,1,2:T(8,128)(2,1)} %bitcast.175) | data formatting | bytes 12582912 | tf_op jit(solution)/shard_map/reshape | solution.py:24
  174.4 66.8 %all-to-all-done = bf16[1536,16,128]{0,2,1:T(8,128)(2,1)} async-done(((bf16[1536,16,128]{0,2,1:T(8,128)(2,1)}), bf16[1536,16,128]{0,2,1:T(8,128)(2,1)}, u32[]{:S(2)}, u32[]{:S(2)}) %all-to-all-start) | async-done | bytes 6291488 | tf_op jit(solution)/shard_map/all_to_all | solution.py:46
  241.2 6.3 copy.822
  247.5 3.5 copy.823
  251.0 9.2 %fusion.11 = f32[8,1536,256]{2,1,0:T(8,128)} fusion(bf16[1536,8,256]{0,1,2:T(8,128)(2,1)S(1)} %bitcast.170, bf16[1,8,256,256]{3,2,1,0:T(8,128)(2,1)S(1)} %copy-done.3), kind=kOutput, calls=%fused_computation.20 | convolution fusion | flops 1610612736 | bytes 19922944 | tf_op jit(solution)/shard_map/tcj,cjn->tcn/dot_general | solution.py:48
  260.2 9.9 %convert_bitcast_fusion.2 = bf16[1536,8,256]{0,2,1:T(8,128)(2,1)} fusion(bf16[1,8,256,256]{3,2,1,0:T(8,128)(2,1)S(1)} %copy-done, f32[8,1536,256]{2,1,0:T(8,128)} %fusion.11), kind=kOutput, calls=%fused_computation.18 | convolution fusion | flops 1642070016 | bytes 19922944 | tf_op jit(solution)/shard_map/tcn,cno->tco/dot_general | solution.py:51
  270.1 12.6 %fusion.6 = bf16[1536,8,256]{2,0,1:T(8,128)(2,1)} fusion(f32[8,1536,256]{2,1,0:T(8,128)} %fusion.11, bf16[1536,8,256]{2,0,1:T(8,128)(2,1)S(1)} %bitcast.181, bf16[1,8,256,256]{3,2,1,0:T(8,128)(2,1)S(1)} %copy-done), kind=kOutput, calls=%fused_computation.8 | convolution fusion | flops 1673527296 | bytes 26214400 | tf_op jit(solution)/shard_map/tco,cno->tcn/dot_general | solution.py:81
  282.7 7.2 convert_bitcast_fusion
  290.0 13.5 %reshape.57 = bf16[1536,8,16,8,2]{0,4,3,2,1:T(2,128)(2,1)} reshape(bf16[1536,8,256]{0,2,1:T(8,128)(2,1)} %convert_bitcast_fusion) | data formatting | bytes 12582912 | tf_op jit(solution)/shard_map/reshape | solution.py:16
  303.5 12.1 %copy.839 = bf16[1536,8,16,8,2]{0,2,4,3,1:T(8,128)(2,1)} copy(bf16[1536,8,16,8,2]{0,4,3,2,1:T(2,128)(2,1)} %reshape.57) | data formatting | bytes 12582912 | tf_op jit(solution)/shard_map/reshape | solution.py:16
  315.5 13.3 %reshape.51 = bf16[1536,8,16,8,2]{0,4,3,2,1:T(2,128)(2,1)} reshape(bf16[1536,8,256]{0,2,1:T(8,128)(2,1)} %convert_bitcast_fusion.2) | data formatting | bytes 12582912 | tf_op jit(solution)/shard_map/reshape | solution.py:16
  328.8 9.5 %copy.826 = bf16[1536,8,16,8,2]{0,2,4,3,1:T(8,128)(2,1)S(1)} copy(bf16[1536,8,16,8,2]{0,4,3,2,1:T(2,128)(2,1)} %reshape.51) | data formatting | bytes 12582912 | tf_op jit(solution)/shard_map/reshape | solution.py:16
  338.3 6.1 copy.827
  344.4 12.1 %all-to-all-start.1 = ((bf16[1536,16,128]{0,2,1:T(8,128)(2,1)}), bf16[1536,16,128]{0,2,1:T(8,128)(2,1)}, u32[]{:S(2)}, u32[]{:S(2)}) async-start(bf16[1536,16,128]{0,2,1:T(8,128)(2,1)} %copy.827), calls=%async_computation.1 | async-start | bytes 12582912 | tf_op jit(solution)/shard_map/all_to_all | solution.py:56
  356.5 24.9 %fusion.34 = (bf16[1536,1,128]{0,1,2:T(2,128)(2,1)}, bf16[1536,1,128]{0,1,2:T(2,128)(2,1)}, bf16[1536,1,128]{0,1,2:T(2,128)(2,1)}, bf16[1536,1,128]{0,1,2:T(2,12...) fusion(bf16[1536,16,128]{0,1,2:T(8,128)(2,1)} %bitcast.169), kind=kLoop, calls=%fused_computation.60 | loop fusion | bytes 12582912 | tf_op jit(solution)/shard_map/split | solution.py:94
  381.4 2.9 copy.843
  384.3 2.9 copy.842
  387.2 2.9 copy.841
  390.1 2.9 copy.840
  400.0 2.9 copy.855
  402.9 2.9 copy.854
  405.8 2.9 copy.853
  408.7 2.9 copy.852
  411.5 2.9 copy.851
  414.4 2.9 copy.850
  417.3 2.9 copy.849
  420.1 2.9 copy.848
  445.2 11.4 %all-to-all-start.3 = ((bf16[16,1536,1,128]{3,1,2,0:T(8,128)(2,1)}), bf16[16,1536,1,128]{3,1,2,0:T(8,128)(2,1)}, u32[]{:S(2)}, u32[]{:S(2)}) async-start(bf16[16,1536,1,128]{3,1,2,0:T(8,128)(2,1)} %bitcast_dynamic-update-slice_fusion), calls=%async_computation.3 | async-start | bytes 12582912 | tf_op jit(solution)/shard_map/all_to_all | solution.py:93
  457.1 8.2 %fusion.17 = f32[1,8,256,256]{3,2,1,0:T(8,128)} fusion(bf16[1536,8,256]{2,0,1:T(8,128)(2,1)} %fusion.6, bf16[1536,8,256]{0,1,2:T(8,128)(2,1)} %bitcast.171), kind=kOutput, calls=%fused_computation.28 | convolution fusion | flops 1610612736 | bytes 14680064 | tf_op jit(solution)/shard_map/tcj,tcn->cjn/dot_general | solution.py:86
  465.3 12.4 %convolution_bitcast_fusion.3 = f32[1,8,256,256]{3,2,1,0:T(8,128)} fusion(bf16[1536,8,256]{2,0,1:T(8,128)(2,1)} %copy.838, f32[8,1536,256]{2,1,0:T(8,128)} %fusion.11), kind=kOutput, calls=%fused_computation.30 | convolution fusion | flops 1638924288 | bytes 20971520 | tf_op jit(solution)/shard_map/tcn,tco->cno/dot_general | solution.py:83
  477.7 6.3 copy.828
  484.0 7.3 copy.829
  491.3 13.7 %reshape_reshape.18 = bf16[1536,2,4,256]{0,3,2,1:T(8,128)(2,1)} reshape(bf16[1536,8,16,8,2]{0,4,3,2,1:T(2,128)(2,1)} %copy.829) | data formatting | bytes 12582912 | tf_op jit(solution)/shard_map/reshape;reshape | solution.py:61
  505.1 5.9 convolution_bitcast_fusion.2
  511.0 34.2 %all-to-all-done.3 = bf16[16,1536,1,128]{3,1,2,0:T(8,128)(2,1)} async-done(((bf16[16,1536,1,128]{3,1,2,0:T(8,128)(2,1)}), bf16[16,1536,1,128]{3,1,2,0:T(8,128)(2,1)}, u32[]{:S(2)}, u32[]{:S(2)}) %all-to-all-start.3) | async-done | bytes 6291488 | tf_op jit(solution)/shard_map/all_to_all | solution.py:93
  545.2 9.1 %copy.856 = bf16[1536,16,1,128]{0,1,3,2:T(8,128)(2,1)} copy(bf16[1536,16,1,128]{3,0,2,1:T(8,128)(2,1)} %bitcast.49) | data formatting | bytes 12582912 | tf_op jit(solution)/shard_map/reshape | solution.py:92
  554.2 12.7 %copy.857 = bf16[1536,8,16,8,2]{0,4,3,2,1:T(2,128)(2,1)} copy(bf16[1536,8,16,8,2]{0,2,4,1,3:T(8,128)(2,1)} %bitcast.179) | data formatting | bytes 12582912 | tf_op jit(solution)/shard_map/transpose | solution.py:24
  566.9 13.7 %reshape_reshape.21 = bf16[1536,2,4,256]{0,3,2,1:T(8,128)(2,1)} reshape(bf16[1536,8,16,8,2]{0,4,3,2,1:T(2,128)(2,1)} %copy.857) | data formatting | bytes 12582912 | tf_op jit(solution)/shard_map/reshape;reshape | solution.py:103
  580.7 5.9 convolution_bitcast_fusion.4
  587.8 4.6 fusion.15
  594.0 3.6 collective-permute-start
  597.6 6.1 fusion.16
  603.7 2.8 copy.859
  607.8 22.9 %collective-permute-done = bf16[1,1536,512]{2,1,0:T(8,128)(2,1)S(1)} collective-permute-done((bf16[1,1536,512]{2,1,0:T(8,128)(2,1)}, bf16[1,1536,512]{2,1,0:T(8,128)(2,1)S(1)}, u32[]{:S(2)}, u32[]{:S(2)}) %collective-permute-start) | collective-permute-done | bytes 1572896 | tf_op jit(solution)/shard_map/ppermute | solution.py:10
  630.7 13.1 %collective-permute-done.1 = bf16[1,1536,512]{2,1,0:T(8,128)(2,1)} collective-permute-done((bf16[1,1536,512]{2,1,0:T(8,128)(2,1)}, bf16[1,1536,512]{2,1,0:T(8,128)(2,1)}, u32[]{:S(2)}, u32[]{:S(2)}) %collective-permute-start.1) | collective-permute-done | bytes 1572896 | tf_op jit(solution)/shard_map/ppermute | solution.py:10
  643.8 158.1 %all-reduce.3.cloned.1.call-done = (f32[1,2,4,256,256]{3,4,2,1,0:T(8,128)}, f32[1,8,256,256]{3,2,1,0:T(8,128)}, f32[1,8,256,256]{3,2,1,0:T(8,128)}, f32[1,2,4,256,256]{4,3,2,1,0:T(8,128)}) async-done(((f32[1,2,4,256,256]{3,4,2,1,0:T(8,128)}, f32[1,8,256,256]{3,2,1,0:T(8,128)}, f32[1,8,256,256]{3,2,1,0:T(8,128)}, f32[1,2,4,256,256]{4,3,2,1,0:T(8,128)}), (f32[1,2,4,256,256]{3,4,2,1,0:T(8,128)}, ...) | async-done | bytes 8388624 | tf_op jit(solution)/shard_map/psum | solution.py:115
  801.9 3.0 copy.865
  804.9 2.8 copy.921
  807.7 2.8 copy.922
  (67 shorter events, 37.8 us)
Async XLA Ops:
  7.2 253.1 %copy-start = (bf16[1,8,256,256]{3,2,1,0:T(8,128)(2,1)S(1)}, bf16[1,8,256,256]{3,2,1,0:T(8,128)(2,1)}, u32[]{:S(2)}) copy-start(bf16[1,8,256,256]{3,2,1,0:T(8,128)(2,1)} %param.10) | copy-start | bytes 3145732
  9.6 19.6 %copy-start.4 = (bf16[1536,2,256]{2,1,0:T(2,128)(2,1)}, bf16[1536,2,256]{2,1,0:T(2,128)(2,1)S(1)}, u32[]{:S(2)}) copy-start(bf16[1536,2,256]{2,1,0:T(2,128)(2,1)S(1)} %reshape_squeeze.7) | copy-start | bytes 4718596
  44.8 95.7 %all-to-all-start.2 = ((bf16[1536,16,128]{0,2,1:T(8,128)(2,1)}), bf16[1536,16,128]{0,2,1:T(8,128)(2,1)}, u32[]{:S(2)}, u32[]{:S(2)}) async-start(bf16[1536,16,128]{0,2,1:T(8,128)(2,1)} %copy.835), calls=%async_computation.2 | async-start | bytes 12582912 | tf_op jit(solution)/shard_map/all_to_all | solution.py:79
  54.4 19.6 %copy-start.6 = (bf16[1536,2,256]{2,1,0:T(2,128)(2,1)}, bf16[1536,2,256]{2,1,0:T(2,128)(2,1)S(1)}, u32[]{:S(2)}) copy-start(bf16[1536,2,256]{2,1,0:T(2,128)(2,1)S(1)} %reshape_squeeze.6) | copy-start | bytes 4718596
  140.5 100.7 %all-to-all-start = ((bf16[1536,16,128]{0,2,1:T(8,128)(2,1)}), bf16[1536,16,128]{0,2,1:T(8,128)(2,1)}, u32[]{:S(2)}, u32[]{:S(2)}) async-start(bf16[1536,16,128]{0,2,1:T(8,128)(2,1)} %copy.821), calls=%async_computation | async-start | bytes 12582912 | tf_op jit(solution)/shard_map/all_to_all | solution.py:46
  247.4 3.5 copy-start.3
  250.9 9.3 %copy-start.2 = (bf16[1536,8,16,8,2]{0,1,4,3,2:T(8,128)(2,1)}, bf16[1536,8,16,8,2]{0,1,4,3,2:T(8,128)(2,1)S(1)}, u32[]{:S(2)}) copy-start(bf16[1536,8,16,8,2]{0,1,4,3,2:T(8,128)(2,1)S(1)} %copy.823) | copy-start | bytes 18874372
  251.0 19.1 %slice-start = ((s8[6291456]{0:T(1024)(128)(4,1)}), s8[4194304]{0:T(1024)(128)(4,1)S(1)}, s32[]{:S(2)}) async-start(s8[6291456]{0:T(1024)(128)(4,1)} %bitcast.180), calls=%async_computation.5 | async-start | bytes 8388608
  260.2 9.9 %slice-start.1 = ((s8[6291456]{0:T(1024)(128)(4,1)}), s8[2097152]{0:T(1024)(128)(4,1)S(1)}, s32[]{:S(2)}) async-start(s8[6291456]{0:T(1024)(128)(4,1)} %bitcast.180), calls=%async_computation.6 | async-start | bytes 4194304
  344.4 100.8 %all-to-all-start.1 = ((bf16[1536,16,128]{0,2,1:T(8,128)(2,1)}), bf16[1536,16,128]{0,2,1:T(8,128)(2,1)}, u32[]{:S(2)}, u32[]{:S(2)}) async-start(bf16[1536,16,128]{0,2,1:T(8,128)(2,1)} %copy.827), calls=%async_computation.1 | async-start | bytes 12582912 | tf_op jit(solution)/shard_map/all_to_all | solution.py:56
  424.7 18.9 %copy-start.13 = (bf16[1536,1,128]{2,0,1:T(8,128)(2,1)S(1)}, bf16[1536,1,128]{2,0,1:T(8,128)(2,1)}, u32[]{:S(2)}) copy-start(bf16[1536,1,128]{2,0,1:T(8,128)(2,1)} %copy.854) | copy-start | bytes 1179652
  424.7 19.7 %copy-start.12 = (bf16[1536,1,128]{2,0,1:T(8,128)(2,1)S(1)}, bf16[1536,1,128]{2,0,1:T(8,128)(2,1)}, u32[]{:S(2)}) copy-start(bf16[1536,1,128]{2,0,1:T(8,128)(2,1)} %copy.855) | copy-start | bytes 1179652
  426.4 10.2 %copy-start.15 = (bf16[1536,1,128]{2,0,1:T(8,128)(2,1)S(1)}, bf16[1536,1,128]{2,0,1:T(8,128)(2,1)}, u32[]{:S(2)}) copy-start(bf16[1536,1,128]{2,0,1:T(8,128)(2,1)} %copy.849) | copy-start | bytes 1179652
  426.4 11.0 %copy-start.14 = (bf16[1536,1,128]{2,0,1:T(8,128)(2,1)S(1)}, bf16[1536,1,128]{2,0,1:T(8,128)(2,1)}, u32[]{:S(2)}) copy-start(bf16[1536,1,128]{2,0,1:T(8,128)(2,1)} %copy.850) | copy-start | bytes 1179652
  445.2 100.0 %all-to-all-start.3 = ((bf16[16,1536,1,128]{3,1,2,0:T(8,128)(2,1)}), bf16[16,1536,1,128]{3,1,2,0:T(8,128)(2,1)}, u32[]{:S(2)}, u32[]{:S(2)}) async-start(bf16[16,1536,1,128]{3,1,2,0:T(8,128)(2,1)} %bitcast_dynamic-update-slice_fusion), calls=%async_computation.3 | async-start | bytes 12582912 | tf_op jit(solution)/shard_map/all_to_all | solution.py:93
  456.6 345.2 %all-reduce.3.cloned.1.call-start = ((), (), s32[]{:S(2)}) async-start(), calls=%async_computation.4 | async-start | bytes 16777216 | tf_op jit(solution)/shard_map/psum | solution.py:115
  491.3 13.7 %copy-start.5 = (bf16[1536,2,256]{2,1,0:T(2,128)(2,1)S(1)}, bf16[1536,2,256]{2,1,0:T(2,128)(2,1)}, u32[]{:S(2)}) copy-start(bf16[1536,2,256]{2,1,0:T(2,128)(2,1)} %copy-done.4) | copy-start | bytes 4718596
  566.9 13.7 %copy-start.7 = (bf16[1536,2,256]{2,1,0:T(2,128)(2,1)S(1)}, bf16[1536,2,256]{2,1,0:T(2,128)(2,1)}, u32[]{:S(2)}) copy-start(bf16[1536,2,256]{2,1,0:T(2,128)(2,1)} %copy-done.6) | copy-start | bytes 4718596
  586.6 1.2 copy-start.16
  594.0 36.7 %collective-permute-start = (bf16[1,1536,512]{2,1,0:T(8,128)(2,1)}, bf16[1,1536,512]{2,1,0:T(8,128)(2,1)S(1)}, u32[]{:S(2)}, u32[]{:S(2)}) collective-permute-start(bf16[1,1536,512]{2,1,0:T(8,128)(2,1)} %copy.832), channel_id=1, source_target_pairs={{0,16},{16,32},{32,48},{1,17},{17,33},{33,49},{2,18},{18,34},{34,5... | collective-permute-start | bytes 4718600 | tf_op jit(solution)/shard_map/ppermute | solution.py:10
  606.5 37.3 %collective-permute-start.1 = (bf16[1,1536,512]{2,1,0:T(8,128)(2,1)}, bf16[1,1536,512]{2,1,0:T(8,128)(2,1)}, u32[]{:S(2)}, u32[]{:S(2)}) collective-permute-start(bf16[1,1536,512]{2,1,0:T(8,128)(2,1)} %copy.859), channel_id=1, source_target_pairs={{16,0},{32,16},{48,32},{17,1},{33,17},{49,33},{18,2},{34,18},{50,3... | collective-permute-start | bytes 4718600 | tf_op jit(solution)/shard_map/ppermute | solution.py:10
  630.7 13.1 %copy-start.11 = (bf16[1,1536,512]{2,1,0:T(8,128)(2,1)}, bf16[1,1536,512]{2,1,0:T(8,128)(2,1)S(1)}, u32[]{:S(2)}) copy-start(bf16[1,1536,512]{2,1,0:T(8,128)(2,1)S(1)} %collective-permute-done) | copy-start | bytes 4718596
  801.9 8.6 %copy-start.10 = (f32[1,8,256,256]{3,2,1,0:T(8,128)S(1)}, f32[1,8,256,256]{3,2,1,0:T(8,128)}, u32[]{:S(2)}) copy-start(f32[1,8,256,256]{3,2,1,0:T(8,128)} %get-tuple-element.143) | copy-start | bytes 6291460
  804.9 6.9 copy-start.9
  807.7 5.5 copy-start.8
  807.7 6.8 copy-start.1
Sparse Core Ops, SparseCore 0:
  586.7 215.1 all-reduce.2
